TPU v7x, 32 devices: a whole 2x2x4 slice. The times are simulated.
32 devices in a mesh: node: 4 (over x, core), src: 8 (over z, y).
Axes of the slice: x: 2, y: 2, z: 4, core: 2. Of those that a mesh axis runs over, the one named last changes fastest.
Arguments:
- transfer: bfloat16 [306, 61440], P(None, 'node'), may hold values from -0.0234375 to 0.0234375
- node_pos: float32 [3, 61440], P(None, 'node'), may hold values from -1 to 1
- node_layer: int32 [61440], P('node'), may hold values from 0 to 2
- layer_cond: float32 [3], replicated, may hold values from 0.3 to 3
- tile_center: float32 [3, 64], replicated, may hold values from -0.6 to 0.6
- dip_tile: int32 [2048], P('src'), may hold values from 0 to 63
- dip_offset: float32 [3, 2048], P(None, 'src'), may hold values from -0.25 to 0.25
- recording: bfloat16 [306, 12288], P(None, ('node', 'src')), may hold values from -165 to 165, as said below
Outputs:
- sources: bfloat16 [3, 2048, 12288], P(None, 'src', 'node')
Inputs may be any that keep to these rules, and one draw needn't show every extreme that they name: `recording`: each sensor has its own gain and offset; the draws stay within the range.
All inputs are finite; a program needn't handle non-finite values.
Results may differ from a plain program's by a relative error of at most 0.0078.
Values may be sent and summed in bfloat16 or wider, within the bound.
A program may use at most 128 MiB of HBM per device.

v0:
```python
import math

import jax
import jax.numpy as jnp
from jax import lax
from jax.sharding import PartitionSpec as P

SOFTENING = 0.02
COV_RIDGE = 0.05
GRAM_RIDGE = 0.01
EPSILON = 1e-06


def place_dipoles(tile_center, dip_tile, dip_offset):
    tile_ids = jnp.arange(tile_center.shape[1], dtype=jnp.int32)
    onehot = (tile_ids[:, None] == dip_tile[None, :]).astype(jnp.float32)
    return jnp.dot(tile_center, onehot, precision=lax.Precision.HIGHEST) + dip_offset


def layer_scale(node_layer, layer_cond):
    levels = jnp.arange(layer_cond.shape[0], dtype=jnp.int32)
    onehot = (node_layer[None, :] == levels[:, None]).astype(jnp.float32)
    return jnp.sum(layer_cond[:, None] * onehot, axis=0)


def potential_block(node_block, scales, dip_pos):
    offsets = node_block[:, :, None] - dip_pos[:, None, :]
    squared = jnp.sum(offsets * offsets, axis=0) + SOFTENING
    weights = scales[:, None] / (squared * jnp.sqrt(squared))
    return jnp.concatenate(
        [offsets[0] * weights, offsets[1] * weights, offsets[2] * weights], axis=1
    ).astype(jnp.bfloat16)


def lead_partial(transfer, node_pos, scales, dip_pos):
    node_rows = transfer.shape[1]
    block_rows = math.gcd(node_rows, 3072)

    def advance(carry, position):
        first_row = position * block_rows
        node_block = lax.dynamic_slice_in_dim(node_pos, first_row, block_rows, 1)
        scale_block = lax.dynamic_slice_in_dim(scales, first_row, block_rows, 0)
        transfer_block = lax.dynamic_slice_in_dim(transfer, first_row, block_rows, 1)
        potential = potential_block(node_block, scale_block, dip_pos)
        return (
            carry + jnp.dot(transfer_block, potential, preferred_element_type=jnp.float32),
            None,
        )

    start_value = jnp.zeros((transfer.shape[0], 3 * dip_pos.shape[1]), jnp.float32)
    result, _ = lax.scan(advance, start_value, jnp.arange(node_rows // block_rows, dtype=jnp.int32))
    return result


def invert_three(matrix):

    def entry(row_index, col_index):
        return matrix[row_index % 3, col_index % 3]

    cofactor = [
        [
            entry(row_index + 1, col_index + 1) * entry(row_index + 2, col_index + 2)
            - entry(row_index + 1, col_index + 2) * entry(row_index + 2, col_index + 1)
            for col_index in range(3)
        ]
        for row_index in range(3)
    ]
    determinant = (
        matrix[0, 0] * cofactor[0][0]
        + matrix[0, 1] * cofactor[0][1]
        + matrix[0, 2] * cofactor[0][2]
    )
    return jnp.stack(
        [
            jnp.stack([cofactor[col_index][row_index] / determinant for col_index in range(3)])
            for row_index in range(3)
        ]
    )


def make_filters(leadfield, cross_sum, sample_sum, sample_count):
    sensors = leadfield.shape[0]
    mean_square = jnp.mean(leadfield * leadfield, axis=(0, 1))
    normed = leadfield / jnp.sqrt(mean_square + EPSILON)[None, None, :]
    average = sample_sum / sample_count
    covariance = (cross_sum - sample_count * jnp.outer(average, average)) / (sample_count - 1.0)
    covariance = covariance + COV_RIDGE * jnp.trace(covariance) / sensors * jnp.eye(
        sensors, dtype=jnp.float32
    )
    factor = jnp.linalg.cholesky(covariance)
    flat = normed.reshape(sensors, -1)
    middle = lax.linalg.triangular_solve(factor, flat, left_side=True, lower=True)
    solved = lax.linalg.triangular_solve(
        factor, middle, left_side=True, lower=True, transpose_a=True
    )
    solved = solved.reshape(normed.shape)
    gram_matrix = jnp.einsum("mcj,mdj->cdj", normed, solved, precision=lax.Precision.HIGHEST)
    ridge_term = GRAM_RIDGE * (gram_matrix[0, 0] + gram_matrix[1, 1] + gram_matrix[2, 2]) / 3.0
    gram_matrix = (
        gram_matrix + ridge_term[None, None, :] * jnp.eye(3, dtype=jnp.float32)[:, :, None]
    )
    inverse = invert_three(gram_matrix)
    filters = jnp.einsum("cdj,mdj->mcj", inverse, solved, precision=lax.Precision.HIGHEST)
    return filters.astype(jnp.bfloat16)


def local(transfer, node_pos, node_layer, layer_cond, tile_center, dip_tile, dip_offset, recording):
    sensors = transfer.shape[0]
    dipoles = dip_tile.shape[0]
    sample_count = float(recording.shape[1] * lax.axis_size("node") * lax.axis_size("src"))
    cross_local = jnp.dot(recording, recording.T, preferred_element_type=jnp.float32)
    sum_local = jnp.sum(recording.astype(jnp.float32), axis=1)
    cross_sum, sample_sum = lax.psum((cross_local, sum_local), ("node", "src"))
    dip_pos = place_dipoles(tile_center, dip_tile, dip_offset)
    scales = layer_scale(node_layer, layer_cond)
    partial_lead = lead_partial(transfer, node_pos, scales, dip_pos).reshape(sensors, 3, dipoles)
    leadfield = lax.psum_scatter(partial_lead, "node", scatter_dimension=2, tiled=True)
    own_filters = make_filters(leadfield, cross_sum, sample_sum, sample_count)
    filters = lax.all_gather(own_filters, "node", axis=2, tiled=True)
    return jnp.einsum(
        "mcj,mt->cjt",
        filters,
        lax.all_gather(recording, "src", axis=1, tiled=True),
        preferred_element_type=jnp.float32,
    ).astype(jnp.bfloat16)


def solution(mesh):
    return jax.shard_map(
        local,
        mesh=mesh,
        in_specs=(
            P(None, "node"),
            P(None, "node"),
            P("node"),
            P(),
            P(),
            P("src"),
            P(None, "src"),
            P(None, ("node", "src")),
        ),
        out_specs=P(None, "src", "node"),
        check_vma=False,
    )
```

profile of v0, /device:TPU:0, one launch (start us, length us, event | category | flops | bytes accessed | tf_op | source)
XLA Modules:
  0.0 281.0 jit_solution(9145742095894084677)
XLA Ops:
  7.4 2.2 fusion.80
  11.6 58.5 %while.13 = (s32[]{:T(128)}, f32[306,768]{1,0:T(8,128)}, s32[5]{0:T(128)S(1)}, bf16[306,15360]{1,0:T(8,128)(2,1)}, f32[3,15360]{1,0:T(4,128)}, /*index=5*/f32[3,...) while((s32[]{:T(128)}, f32[306,768]{1,0:T(8,128)}, ...), condition=%wide.region_13.14_spmd.clone, body=%wide.region_11.13_spmd.clone.sunk | while | flops 1471884288 | bytes 38569156 | solution.py:51
  15.4 3.1 %fusion.102 = (bf16[3072,256]{1,0:T(8,128)(2,1)S(1)}, bf16[3072,256]{1,0:T(8,128)(2,1)S(1)}, bf16[3072,256]{1,0:T(8,128)(2,1)}) fusion(f32[3,3072,256]{2,1,0:T(8,128)S(1)} %get-tuple-element.217, f32[3072,256]{1,0:T(8,128)S(1)} %get-tuple-element.218, f32[3072]{0:T(1024)S(1)} %dynamic_slice.29), kind=kLoop, calls=%fused_computation.20.clone.1 | loop fusion | flops 7077888 | bytes 17313792 | tf_op jit(solution)/shard_map/convert.4
  18.5 4.6 %select_add_fusion.3 = f32[306,768]{1,0:T(8,128)} fusion(f32[306,768]{1,0:T(8,128)} %get-tuple-element.234, bf16[3072,256]{1,0:T(8,128)(2,1)} %get-tuple-element.219, bf16[3072,256]{1,0:T(8,128)(2,1)S(1)} %get-tuple-element.220, bf16[3072,256]{1,0:T(8,128)(2,1)S(1)} %get-tuple-element.221, bf16[306,15360]{1,0:T(8,128)(2,1)} %get-tuple-element.247, ...), kind=kOutput, calls=%fused_computation.22.clone.1 | convolution fusion | flops 1458514944 | bytes 8534021 | tf_op jit(solution)/shard_map/while/body/eval_jaxpr/dot_general | solution.py:46
  26.8 3.1 %fusion.102 = (bf16[3072,256]{1,0:T(8,128)(2,1)S(1)}, bf16[3072,256]{1,0:T(8,128)(2,1)S(1)}, bf16[3072,256]{1,0:T(8,128)(2,1)}) fusion(f32[3,3072,256]{2,1,0:T(8,128)S(1)} %get-tuple-element.217, f32[3072,256]{1,0:T(8,128)S(1)} %get-tuple-element.218, f32[3072]{0:T(1024)S(1)} %dynamic_slice.29), kind=kLoop, calls=%fused_computation.20.clone.1 | loop fusion | flops 7077888 | bytes 17313792 | tf_op jit(solution)/shard_map/convert.4
  29.9 4.9 %select_add_fusion.3 = f32[306,768]{1,0:T(8,128)} fusion(f32[306,768]{1,0:T(8,128)} %get-tuple-element.234, bf16[3072,256]{1,0:T(8,128)(2,1)} %get-tuple-element.219, bf16[3072,256]{1,0:T(8,128)(2,1)S(1)} %get-tuple-element.220, bf16[3072,256]{1,0:T(8,128)(2,1)S(1)} %get-tuple-element.221, bf16[306,15360]{1,0:T(8,128)(2,1)} %get-tuple-element.247, ...), kind=kOutput, calls=%fused_computation.22.clone.1 | convolution fusion | flops 1458514944 | bytes 8534021 | tf_op jit(solution)/shard_map/while/body/eval_jaxpr/dot_general | solution.py:46
  38.6 3.1 %fusion.102 = (bf16[3072,256]{1,0:T(8,128)(2,1)S(1)}, bf16[3072,256]{1,0:T(8,128)(2,1)S(1)}, bf16[3072,256]{1,0:T(8,128)(2,1)}) fusion(f32[3,3072,256]{2,1,0:T(8,128)S(1)} %get-tuple-element.217, f32[3072,256]{1,0:T(8,128)S(1)} %get-tuple-element.218, f32[3072]{0:T(1024)S(1)} %dynamic_slice.29), kind=kLoop, calls=%fused_computation.20.clone.1 | loop fusion | flops 7077888 | bytes 17313792 | tf_op jit(solution)/shard_map/convert.4
  41.7 4.9 %select_add_fusion.3 = f32[306,768]{1,0:T(8,128)} fusion(f32[306,768]{1,0:T(8,128)} %get-tuple-element.234, bf16[3072,256]{1,0:T(8,128)(2,1)} %get-tuple-element.219, bf16[3072,256]{1,0:T(8,128)(2,1)S(1)} %get-tuple-element.220, bf16[3072,256]{1,0:T(8,128)(2,1)S(1)} %get-tuple-element.221, bf16[306,15360]{1,0:T(8,128)(2,1)} %get-tuple-element.247, ...), kind=kOutput, calls=%fused_computation.22.clone.1 | convolution fusion | flops 1458514944 | bytes 8534021 | tf_op jit(solution)/shard_map/while/body/eval_jaxpr/dot_general | solution.py:46
  50.3 3.1 %fusion.102 = (bf16[3072,256]{1,0:T(8,128)(2,1)S(1)}, bf16[3072,256]{1,0:T(8,128)(2,1)S(1)}, bf16[3072,256]{1,0:T(8,128)(2,1)}) fusion(f32[3,3072,256]{2,1,0:T(8,128)S(1)} %get-tuple-element.217, f32[3072,256]{1,0:T(8,128)S(1)} %get-tuple-element.218, f32[3072]{0:T(1024)S(1)} %dynamic_slice.29), kind=kLoop, calls=%fused_computation.20.clone.1 | loop fusion | flops 7077888 | bytes 17313792 | tf_op jit(solution)/shard_map/convert.4
  53.4 4.9 %select_add_fusion.3 = f32[306,768]{1,0:T(8,128)} fusion(f32[306,768]{1,0:T(8,128)} %get-tuple-element.234, bf16[3072,256]{1,0:T(8,128)(2,1)} %get-tuple-element.219, bf16[3072,256]{1,0:T(8,128)(2,1)S(1)} %get-tuple-element.220, bf16[3072,256]{1,0:T(8,128)(2,1)S(1)} %get-tuple-element.221, bf16[306,15360]{1,0:T(8,128)(2,1)} %get-tuple-element.247, ...), kind=kOutput, calls=%fused_computation.22.clone.1 | convolution fusion | flops 1458514944 | bytes 8534021 | tf_op jit(solution)/shard_map/while/body/eval_jaxpr/dot_general | solution.py:46
  62.1 3.1 %fusion.102 = (bf16[3072,256]{1,0:T(8,128)(2,1)S(1)}, bf16[3072,256]{1,0:T(8,128)(2,1)S(1)}, bf16[3072,256]{1,0:T(8,128)(2,1)}) fusion(f32[3,3072,256]{2,1,0:T(8,128)S(1)} %get-tuple-element.217, f32[3072,256]{1,0:T(8,128)S(1)} %get-tuple-element.218, f32[3072]{0:T(1024)S(1)} %dynamic_slice.29), kind=kLoop, calls=%fused_computation.20.clone.1 | loop fusion | flops 7077888 | bytes 17313792 | tf_op jit(solution)/shard_map/convert.4
  65.2 4.9 %select_add_fusion.3 = f32[306,768]{1,0:T(8,128)} fusion(f32[306,768]{1,0:T(8,128)} %get-tuple-element.234, bf16[3072,256]{1,0:T(8,128)(2,1)} %get-tuple-element.219, bf16[3072,256]{1,0:T(8,128)(2,1)S(1)} %get-tuple-element.220, bf16[3072,256]{1,0:T(8,128)(2,1)S(1)} %get-tuple-element.221, bf16[306,15360]{1,0:T(8,128)(2,1)} %get-tuple-element.247, ...), kind=kOutput, calls=%fused_computation.22.clone.1 | convolution fusion | flops 1458514944 | bytes 8534021 | tf_op jit(solution)/shard_map/while/body/eval_jaxpr/dot_general | solution.py:46
  74.2 42.8 %psum.15 = f32[306]{0:T(512)S(1)} all-reduce(f32[306]{0:T(512)S(1)} %convert_reduce_fusion), channel_id=1, replica_groups=mesh['node'=4,'src'=8] {'node','src'}, use_global_device_ids=true, to_apply=%region_2.0 | all-reduce | flops 306 | bytes 2448 | tf_op jit(solution)/shard_map/psum | solution.py:113
  118.4 38.9 %all-reduce.7.cloned.1.call-done = f32[306,306]{1,0:T(8,128)} async-done(((f32[306,306]{1,0:T(8,128)}), f32[306,306]{1,0:T(8,128)}) %all-reduce.7.cloned.1.call-update) | async-done | bytes 374560 | tf_op jit(solution)/shard_map/psum | solution.py:113
  162.3 11.7 %cholesky.77 = f32[128,128]{1,0:T(8,128)S(1)} custom-call(f32[128,128]{1,0:T(8,128)S(1)} %cholesky.195), custom_call_target="Cholesky" | custom-call | tf_op jit(solution)/shard_map/jit(cholesky)/cholesky | solution.py:90
  174.1 9.8 %custom-call.24 = f32[1,128,128]{1,2,0:T(8,128)S(1)} custom-call(f32[1,128,128]{2,1,0:T(8,128)S(1)} %get-tuple-element.125), custom_call_target="InvertDiagBlocksLowerTriangular" | custom-call | tf_op jit(solution)/shard_map/jit(cholesky)/cholesky | solution.py:90
  184.6 11.7 %cholesky.162 = f32[128,128]{1,0:T(8,128)S(1)} custom-call(f32[128,128]{1,0:T(8,128)S(1)} %cholesky.199), custom_call_target="Cholesky" | custom-call | tf_op jit(solution)/shard_map/jit(cholesky)/cholesky | solution.py:90
  196.3 10.0 %custom-call.25 = f32[1,128,128]{1,2,0:T(8,128)S(1)} custom-call(f32[1,128,128]{2,1,0:T(8,128)S(1)} %get-tuple-element.122), custom_call_target="InvertDiagBlocksLowerTriangular" | custom-call | tf_op jit(solution)/shard_map/jit(cholesky)/cholesky | solution.py:90
  206.7 4.6 %cholesky.184 = f32[50,50]{1,0:T(8,128)S(1)} custom-call(f32[50,50]{1,0:T(8,128)S(1)} %convolution_subtract_fusion.5), custom_call_target="Cholesky" | custom-call | tf_op jit(solution)/shard_map/jit(cholesky)/cholesky | solution.py:90
  214.8 4.2 %while.12 = (s32[]{:T(128)}, f32[306,306]{1,0:T(8,128)S(1)}, s32[2,2]{1,0:T(2,128)S(1)}, f32[2,128,128]{2,1,0:T(8,128)S(1)}, s32[]{:T(128)}) while((s32[]{:T(128)}, f32[306,306]{1,0:T(8,128)S(1)}, s32[2,2]{1,0:T(2,128)S(1)}, f32[2,128,128]{2,1,0:T(8,128)S(1)}, s32[]{:T(128)}) %tuple.72), condition=%wide.while_cond, body=%wide.while_body.sunk | while | flops 2 | bytes 131189 | solution.py:93
  219.1 29.5 %custom-call.26 = f32[3,128,128]{1,2,0:T(8,128)S(1)} custom-call(f32[3,128,128]{2,1,0:T(8,128)S(1)} %pad_maximum_fusion.1), custom_call_target="InvertDiagBlocksLowerTriangular" | custom-call | tf_op jit(solution)/shard_map/triangular_solve | solution.py:93
  253.4 2.3 convolution_bitcast_fusion
  260.2 7.5 %all_gather.6 = bf16[306,3,256]{0,2,1:T(8,128)(2,1)S(1)} all-gather(bf16[306,3,64]{0,2,1:T(8,128)(2,1)S(1)} %copy.93), channel_id=1, replica_groups=mesh['node'=4,'src'=8] {'node'}, dimensions={2}, use_global_device_ids=true | all-gather | bytes 587520 | tf_op jit(solution)/shard_map/all_gather | solution.py:119
  267.7 5.8 %convolution_convert_fusion = bf16[3,256,3072]{2,1,0:T(8,128)(2,1)} fusion(bf16[306,3,256]{0,2,1:T(8,128)(2,1)S(1)} %all_gather.6, bf16[306,3072]{1,0:T(8,128)(2,1)} %all-gather.2.cloned.1.call-done), kind=kOutput, calls=%fused_computation.26 | convolution fusion | flops 1446248448 | bytes 7068672 | tf_op jit(solution)/shard_map/mcj,mt->cjt/dot_general | solution.py:120
  (105 shorter events, 42.7 us)
Async XLA Ops:
  7.4 3.4 %copy-start = (f32[3,64]{1,0:T(4,128)S(1)}, f32[3,64]{1,0:T(4,128)}, u32[]{:S(2)}) copy-start(f32[3,64]{1,0:T(4,128)} %param.14) | copy-start | bytes 2308
  7.4 149.9 %all-reduce.7.cloned.1.call-start = ((), (), s32[]{:S(2)}) async-start(), calls=%async_computation | async-start | bytes 958464 | tf_op jit(solution)/shard_map/psum | solution.py:113
  9.6 239.1 %all-reduce.9.cloned.1.call-start = ((), (), s32[]{:S(2)}) async-start(), calls=%async_computation.2 | async-start | bytes 3145728
  70.1 4.0 %copy-start.1 = (bf16[306,384]{1,0:T(8,128)(2,1)S(1)}, bf16[306,384]{1,0:T(8,128)(2,1)}, u32[]{:S(2)}) copy-start(bf16[306,384]{1,0:T(8,128)(2,1)} %param.17) | copy-start | bytes 705028
  70.1 47.0 %copy-start.2 = (u32[32]{0:T(128)S(1)}, u32[32]{0:T(128)}, u32[]{:S(2)}) copy-start(u32[32]{0:T(128)} %constant.194) | copy-start | bytes 388
  73.4 194.3 %all-gather.2.cloned.1.call-start = ((), (), s32[]{:S(2)}) async-start(), calls=%async_computation.1 | async-start | bytes 2156544 | tf_op jit(solution)/shard_map/all_gather | solution.py:123
Sparse Core Ops, SparseCore 0:
  13.5 143.7 all-reduce.6
  159.7 43.2 all-reduce.8
Sparse Core Ops, SparseCore 1:
  76.0 52.1 all-gather.1
where the time goes:
time: 282 us; the launch traced here: 281 us
  other arithmetic  111 us (39%)
  blocking collectives  50.4 us (18%)
  matrix products  40.1 us (14%)
  waiting for transfers between devices  39.5 us (14%)
  between operations  18.4 us (7%)
  local copies, waits for them, and re-layouts  17.8 us (6%)
  loops' own time  3.42 us (1%)
    another operation x10, other arithmetic, make_filters(): factor = jnp.linalg.cholesky(covariance)  49.3 us
    psum x1, blocking collectives, local(): cross_sum, sample_sum = lax.psum((cross_local, sum_local), ('node', 'src'))  42.8 us
    psum x1, waiting for transfers between devices, local(): cross_sum, sample_sum = lax.psum((cross_local, sum_local), ('node', 'src'))  38.9 us
    another operation x8, other arithmetic, make_filters(): lax.linalg.triangular_solve(factor, middle, left_side=True, lower=True, t...  29.7 us
    dot_general x5, matrix products, advance(): jnp.dot(transfer_block, potential, preferred_element_type=jnp.float32)  24.2 us
    another operation x5, other arithmetic  15.4 us
    reduce_sum x5, other arithmetic, potential_block(): squared = jnp.sum(offsets * offsets, axis=0) + SOFTENING  8.44 us
    all_gather x1, blocking collectives, local(): filters = lax.all_gather(own_filters, 'node', axis=2, tiled=True)  7.51 us
  transfers between devices with their start and end apart: 3, of which 1 were waited for; matrix products, arithmetic and copies ran while one was open for 57% of the time, Pallas kernels for 0%

commit v1 on v0

v1 whole, which is shorter than its diff:
```python
import functools
import math

import jax
import jax.numpy as jnp
from jax import lax
from jax.experimental import pallas as pl
from jax.experimental.pallas import tpu as pltpu
from jax.sharding import PartitionSpec as P

SOFTENING = 0.02
COV_RIDGE = 0.05
GRAM_RIDGE = 0.01
EPSILON = 1e-06
NT = (((1,), (1,)), ((), ()))
F32 = jnp.float32
BF16 = jnp.bfloat16


def round_up(value, unit):
    return -(-value // unit) * unit


def place_dipoles(tile_center, dip_tile, dip_offset):
    tile_ids = jnp.arange(tile_center.shape[1], dtype=jnp.int32)
    onehot = (tile_ids[:, None] == dip_tile[None, :]).astype(F32)
    return jnp.dot(tile_center, onehot, precision=lax.Precision.HIGHEST) + dip_offset


def layer_scale(node_layer, layer_cond):
    levels = jnp.arange(layer_cond.shape[0], dtype=jnp.int32)
    onehot = (node_layer[None, :] == levels[:, None]).astype(F32)
    return jnp.sum(layer_cond[:, None] * onehot, axis=0)


def remote(held, dst, send_sem, recv_sem, **where):
    return pltpu.make_async_remote_copy(
        src_ref=held, dst_ref=dst, send_sem=send_sem, recv_sem=recv_sem,
        device_id=where, device_id_type=pl.DeviceIdType.MESH,
    )


def potential_rows(node, dip, rows):
    dipoles = dip.shape[0]
    parts = [[], [], []]
    for first in range(0, dipoles, rows):
        offsets = [node[c : c + 1, :] - dip[first : first + rows, c : c + 1] for c in range(3)]
        q = offsets[0] * offsets[0] + offsets[1] * offsets[1] + offsets[2] * offsets[2] + SOFTENING
        root = lax.rsqrt(q)
        weights = (node[3:4, :] * root) * (root * root)
        for c in range(3):
            parts[c].append((offsets[c] * weights).astype(BF16))
    return jnp.concatenate(parts[0] + parts[1] + parts[2], axis=0)


def lead_kernel(
    nd, ns, r, stages,
    rec, transfer, node, dip, cross_out, lead_out,
    aug, acc, buf, got_a, part, got_b, fin, res,
    s_a, r_a, s_b, r_b, s_c, r_c, s_d, r_d,
):
    step = pl.program_id(0)
    me_n, me_s = lax.axis_index("node"), lax.axis_index("src")
    sensors = rec.shape[0]
    dipoles = dip.shape[0]
    mp = aug.shape[0]
    peer_n = [None] + [lax.rem(me_n + k, nd) for k in range(1, nd)]
    peer_s = [None] + [lax.rem(me_s + k, ns) for k in range(1, ns)]

    def copy_a(k):
        return remote(buf.at[peer_n[k]], got_a.at[k - 1], s_a.at[k - 1], r_a.at[k - 1], node=peer_n[k])

    def copy_b(k):
        return remote(part.at[peer_s[k]], got_b.at[k - 1], s_b.at[k - 1], r_b.at[k - 1], src=peer_s[k])

    def copy_c(k):
        return remote(fin, res.at[me_n, me_s], s_c.at[k - 1], r_c.at[k - 1], src=peer_s[k])

    def copy_d(k):
        return remote(res.at[me_n], res.at[me_n], s_d.at[k - 1], r_d.at[k - 1], node=peer_n[k])

    @pl.when(step == stages[0])
    def _():
        barrier = pltpu.get_barrier_semaphore()
        for k in range(1, nd):
            pl.semaphore_signal(barrier, inc=1, device_id={"node": peer_n[k]}, device_id_type=pl.DeviceIdType.MESH)
        for k in range(1, ns):
            pl.semaphore_signal(barrier, inc=1, device_id={"src": peer_s[k]}, device_id_type=pl.DeviceIdType.MESH)
        acc[...] = jnp.zeros_like(acc)
        low = sensors // 16 * 16
        tail = lax.broadcasted_iota(jnp.int32, (mp - low, aug.shape[1]), 0) + low
        aug[low:, :] = jnp.where(tail == sensors, 1.0, 0.0).astype(BF16)
        aug[:sensors, :] = rec[...]
        held = aug[...]
        cross = lax.dot_general(held, held, NT, preferred_element_type=F32)
        for n in range(nd):
            for s in range(ns):
                first = (n * ns + s) * r
                buf[n, s] = cross[first : first + r, :]
        pl.semaphore_wait(barrier, nd - 1 + ns - 1)

    @pl.when(step == stages[1])
    def _():
        for k in range(1, nd):
            copy_a(k).start()

    @pl.when(step == stages[2])
    def _():
        total = buf[me_n]
        for k in range(1, nd):
            copy_a(k).wait()
            total = total + got_a[k - 1]
        part[...] = total

    @pl.when(step == stages[3])
    def _():
        for k in range(1, ns):
            copy_b(k).start()

    @pl.when(step == stages[4])
    def _():
        total = part[me_s]
        for k in range(1, ns):
            copy_b(k).wait()
            total = total + got_b[k - 1]
        fin[...] = total
        res[me_n, me_s] = total

    @pl.when(step == stages[5])
    def _():
        for k in range(1, ns):
            copy_c(k).start()

    @pl.when(step == stages[6])
    def _():
        for k in range(1, ns):
            copy_c(k).wait()
        for k in range(1, nd):
            copy_d(k).start()

    block = transfer.shape[1]
    sub = math.gcd(block, 512)
    dip_now = dip[...]
    total = None
    for first in range(0, block, sub):
        potential = potential_rows(node[:, first : first + sub], dip_now, 32)
        product = lax.dot_general(
            transfer[:, first : first + sub], potential, NT, preferred_element_type=F32
        )
        total = product if total is None else total + product
    acc[:sensors, :] += total

    @pl.when(step == stages[7])
    def _():
        flipped = acc[...].T
        own = dipoles // nd
        for n in range(nd):
            for c in range(3):
                first = c * dipoles + n * own
                lead_out[n, c] = flipped[first : first + own, :]
        for k in range(1, nd):
            copy_d(k).wait()
        cross_out[...] = jnp.zeros_like(cross_out)
        for n in range(nd):
            for s in range(ns):
                first = (n * ns + s) * r
                cross_out[first : first + r, :] = res[n, s]


def lead_and_cross(rec, transfer, node, dip):
    nd, ns = lax.axis_size("node"), lax.axis_size("src")
    sensors, time = rec.shape
    nodes = transfer.shape[1]
    dipoles = dip.shape[0]
    mp = round_up(sensors + 1, 128)
    r = -(-(sensors + 1) // (nd * ns))
    block = math.gcd(nodes, 1024)
    steps = nodes // block
    last = steps - 1
    stages = (0, 1, last * 4 // 14, last * 5 // 14, last * 8 // 14, last * 9 // 14, last * 12 // 14, last)
    chunk = (nd, ns, r, mp)
    vmem = pl.BlockSpec(memory_space=pltpu.VMEM)
    return pl.pallas_call(
        functools.partial(lead_kernel, nd, ns, r, stages),
        grid=(steps,),
        out_shape=(
            jax.ShapeDtypeStruct((mp, mp), F32),
            jax.ShapeDtypeStruct((nd, 3, dipoles // nd, mp), F32),
        ),
        in_specs=[
            vmem,
            pl.BlockSpec((sensors, block), lambda i: (0, i)),
            pl.BlockSpec((4, block), lambda i: (0, i)),
            vmem,
        ],
        out_specs=(vmem, vmem),
        scratch_shapes=[
            pltpu.VMEM((mp, time), BF16),
            pltpu.VMEM((mp, 3 * dipoles), F32),
            pltpu.VMEM(chunk, F32),
            pltpu.VMEM((nd - 1,) + chunk[1:], F32),
            pltpu.VMEM(chunk[1:], F32),
            pltpu.VMEM((ns - 1,) + chunk[2:], F32),
            pltpu.VMEM(chunk[2:], F32),
            pltpu.VMEM(chunk, F32),
        ]
        + [pltpu.SemaphoreType.DMA((n,)) for n in (nd - 1, nd - 1, ns - 1, ns - 1, ns - 1, ns - 1, nd - 1, nd - 1)],
        compiler_params=pltpu.CompilerParams(collective_id=0, has_side_effects=True),
        name="lead_cross",
    )(rec, transfer, node, dip)


def dot_full(a, b):
    return jnp.dot(a, b, precision=lax.Precision.HIGHEST, preferred_element_type=F32)


def halves(a):
    high = a.astype(BF16)
    return high, (a - high.astype(F32)).astype(BF16)


def dot_three(a, b):
    (ah, al), (bh, bl) = a, b
    dot = functools.partial(jnp.dot, preferred_element_type=F32)
    return dot(ah, bh) + (dot(ah, bl) + dot(al, bh))


def covariance_inverse(cross, sensors, count, full_steps):
    mp = cross.shape[0]
    rows = lax.broadcasted_iota(jnp.int32, (mp, mp), 0)
    cols = lax.broadcasted_iota(jnp.int32, (mp, mp), 1)
    average = cross[:, sensors : sensors + 1] / count
    sums = cross[sensors : sensors + 1, :]
    cov = (cross - average * sums) / (count - 1.0)
    cov = jnp.where((rows < sensors) & (cols < sensors), cov, 0.0)
    diagonal = rows == cols
    trace = jnp.sum(jnp.sum(jnp.where(diagonal, cov, 0.0), axis=1, keepdims=True), axis=0, keepdims=True)
    ridge = COV_RIDGE / sensors * trace
    centre = 0.5 * trace + ridge
    scaled = cov / centre + jnp.where(diagonal, jnp.where(rows < sensors, ridge / centre, 1.0), 0.0)
    ratio = sensors / COV_RIDGE + 1.0
    h = (ratio - 1.0) / (ratio + 1.0)
    plan = []
    while h > 1e-5:
        plan.append(1.0 / (2.0 - h * h))
        h = h * h / (2.0 - h * h)
    eye = jnp.where(diagonal, 1.0, 0.0)
    x = (4.0 * plan[0]) * eye - (2.0 * plan[0]) * scaled
    scaled_halves = halves(scaled)
    for at, gain in enumerate(plan[1:], 1):
        if at >= len(plan) - full_steps:
            y = dot_full(scaled, x)
            x = dot_full(x, (4.0 * gain) * eye - (2.0 * gain) * y)
        else:
            xh = halves(x)
            y = dot_three(scaled_halves, xh)
            x = dot_three(xh, halves((4.0 * gain) * eye - (2.0 * gain) * y))
    return x / centre


def filter_kernel(
    nd, ns, inner, count,
    cross, lead, rec, filt, rec_all,
    got, s_l, r_l, s_y, r_y, s_z, r_z, s_f, r_f,
):
    me_n, me_s = lax.axis_index("node"), lax.axis_index("src")
    outer = ns // inner
    sensors, time = rec.shape
    own = lead.shape[2]
    mp = cross.shape[0]
    hi, lo = me_s // inner, lax.rem(me_s, inner)
    peer_n = [None] + [lax.rem(me_n + k, nd) for k in range(1, nd)]
    peer_z = [None] + [lax.rem(hi + k, outer) * inner + lo for k in range(1, outer)]
    from_z = [me_s] + [lax.rem(hi + outer - k, outer) * inner + lo for k in range(1, outer)]
    peer_y = hi * inner + lax.rem(lo + 1, inner)

    def columns(s):
        return rec_all.at[:, pl.ds(pl.multiple_of(s * time, time), time)]

    def copy_l(k):
        return remote(lead.at[peer_n[k]], got.at[k - 1], s_l.at[k - 1], r_l.at[k - 1], node=peer_n[k])

    def copy_y(k):
        source = rec if k == 0 else columns(from_z[k])
        return remote(source, columns(from_z[k]), s_y.at[k], r_y.at[k], src=peer_y)

    def copy_z(k):
        return remote(rec, columns(me_s), s_z.at[k - 1], r_z.at[k - 1], src=peer_z[k])

    def copy_f(k):
        return remote(filt.at[:, me_n], filt.at[:, me_n], s_f.at[k - 1], r_f.at[k - 1], node=peer_n[k])

    barrier = pltpu.get_barrier_semaphore()
    for k in range(1, nd):
        pl.semaphore_signal(barrier, inc=1, device_id={"node": peer_n[k]}, device_id_type=pl.DeviceIdType.MESH)
    for k in range(1, outer):
        pl.semaphore_signal(barrier, inc=1, device_id={"src": peer_z[k]}, device_id_type=pl.DeviceIdType.MESH)
    pl.semaphore_signal(barrier, inc=1, device_id={"src": peer_y}, device_id_type=pl.DeviceIdType.MESH)
    pl.semaphore_wait(barrier, nd - 1 + outer)

    for k in range(1, nd):
        copy_l(k).start()
    copy_y(0).start()
    for k in range(1, outer):
        copy_z(k).start()
    rec_all[:, pl.ds(pl.multiple_of(me_s * time, time), time)] = rec[...]

    inverse = covariance_inverse(cross[...], sensors, count, 3)

    for k in range(1, outer):
        copy_z(k).wait()
        copy_y(k).start()
    field = lead[me_n]
    for k in range(1, nd):
        copy_l(k).wait()
        field = field + got[k - 1]
    square = jnp.sum(jnp.sum(field * field, axis=0), axis=1, keepdims=True) / (3.0 * sensors)
    normed = field / jnp.sqrt(square + EPSILON)[None]
    solved = dot_full(normed.reshape(3 * own, mp), inverse).reshape(3, own, mp)
    gram = {}
    for c in range(3):
        for d in range(c, 3):
            gram[c, d] = jnp.sum(normed[c] * solved[d], axis=1, keepdims=True)
            gram[d, c] = gram[c, d]
    ridge = GRAM_RIDGE * (gram[0, 0] + gram[1, 1] + gram[2, 2]) / 3.0
    for c in range(3):
        gram[c, c] = gram[c, c] + ridge

    def cofactor(row, col):
        a, b, c, d = (row + 1) % 3, (row + 2) % 3, (col + 1) % 3, (col + 2) % 3
        return gram[a, c] * gram[b, d] - gram[a, d] * gram[b, c]

    determinant = gram[0, 0] * cofactor(0, 0) + gram[0, 1] * cofactor(0, 1) + gram[0, 2] * cofactor(0, 2)
    for c in range(3):
        mixed = sum((cofactor(d, c) / determinant) * solved[d] for d in range(3))
        filt[c, me_n] = mixed[:, :sensors].astype(BF16)
    for k in range(1, nd):
        copy_f(k).start()
    for k in range(outer):
        copy_y(k).wait()
    for k in range(1, nd):
        copy_f(k).wait()


def make_filters(cross, lead, rec):
    nd, ns = lax.axis_size("node"), lax.axis_size("src")
    sensors, time = rec.shape
    own, mp = lead.shape[2:]
    inner = 2
    outer = ns // inner
    vmem = pl.BlockSpec(memory_space=pltpu.VMEM)
    return pl.pallas_call(
        functools.partial(filter_kernel, nd, ns, inner, float(time * nd * ns)),
        out_shape=(
            jax.ShapeDtypeStruct((3, nd, own, sensors), BF16),
            jax.ShapeDtypeStruct((sensors, ns * time), BF16),
        ),
        in_specs=[vmem] * 3,
        out_specs=(vmem, vmem),
        scratch_shapes=[pltpu.VMEM((nd - 1,) + lead.shape[1:], F32)]
        + [pltpu.SemaphoreType.DMA((n,)) for n in (nd - 1, nd - 1, outer, outer, outer - 1, outer - 1, nd - 1, nd - 1)],
        compiler_params=pltpu.CompilerParams(collective_id=1, has_side_effects=True),
        name="filters",
    )(cross, lead, rec)


def local(transfer, node_pos, node_layer, layer_cond, tile_center, dip_tile, dip_offset, recording):
    sensors = transfer.shape[0]
    dipoles = dip_tile.shape[0]
    dip_pos = place_dipoles(tile_center, dip_tile, dip_offset)
    scales = layer_scale(node_layer, layer_cond)
    node = jnp.concatenate([node_pos, scales[None, :]], axis=0)
    cross, lead = lead_and_cross(recording, transfer, node, dip_pos.T)
    filters, samples = make_filters(cross, lead, recording)
    out = jnp.dot(filters.reshape(3 * dipoles, sensors), samples, preferred_element_type=F32)
    return out.astype(BF16).reshape(3, dipoles, samples.shape[1])


def solution(mesh):
    return jax.shard_map(
        local,
        mesh=mesh,
        in_specs=(
            P(None, "node"),
            P(None, "node"),
            P("node"),
            P(),
            P(),
            P("src"),
            P(None, "src"),
            P(None, ("node", "src")),
        ),
        out_specs=P(None, "src", "node"),
        check_vma=False,
    )
```

time: 282 us -> 92.9 us (0.33)
  other arithmetic: 111 us -> 2.84 us
  Pallas kernels: 0 us -> 80.6 us
  blocking collectives: 50.4 us -> 0 us
  waiting for transfers between devices: 39.5 us -> 0 us
  matrix products: 40.1 us -> 8.12 us
  between operations: 18.4 us -> 0.04 us
  local copies, waits for them, and re-layouts: 17.8 us -> 0.82 us
  loops' own time: 3.42 us -> 0 us
    another operation x27 -> x0, other arithmetic: 94.5 us -> none  [the longest x10 49.3 us: make_filters(): factor = jnp.linalg.cholesky(covariance)]
    pallas_call x0 -> x2, Pallas kernels: none -> 80.6 us  [the longest x1 40.6 us: lead_and_cross(): pl.pallas_call(functools.partial(lead_kernel, nd, ns, r, stages), grid=(s...]
    psum x1 -> x0, blocking collectives: 42.8 us -> none  [local(): cross_sum, sample_sum = lax.psum((cross_local, sum_local), ('node', 'src'))]
    psum x1 -> x0, waiting for transfers between devices: 38.9 us -> none  [local(): cross_sum, sample_sum = lax.psum((cross_local, sum_local), ('node', 'src'))]
    dot_general x9 -> x1, matrix products: 35.6 us -> 6.52 us  [local(): jnp.dot(filters.reshape(3 * dipoles, sensors), samples, preferred_element...]
    reduce_sum x8 -> x0, other arithmetic: 11.9 us -> none  [the longest x5 8.44 us: potential_block(): squared = jnp.sum(offsets * offsets, axis=0) + SOFTENING]
    all_gather x1 -> x0, blocking collectives: 7.51 us -> none  [local(): filters = lax.all_gather(own_filters, 'node', axis=2, tiled=True)]
    dynamic_slice x15 -> x0, local copies, waits for them, and re-layouts: 7.05 us -> none  [the longest x5 4.07 us: advance(): node_block = lax.dynamic_slice_in_dim(node_pos, first_row, block_rows, 1)]
  transfers between devices with their start and end apart: 3 -> 0, of which waited for: 1 -> 0; matrix products, arithmetic and copies ran while one was open for 57% -> 0% of each run, Pallas kernels for 0% -> 0%
where the time goes in v1:
time: 92.9 us; the launch traced here: 92.4 us
  Pallas kernels  80.6 us (87%)
  matrix products  8.12 us (9%)
  other arithmetic  2.84 us (3%)
    pallas_call x1, Pallas kernels, lead_and_cross(): pl.pallas_call(functools.partial(lead_kernel, nd, ns, r, stages), grid=(s...  40.6 us
    pallas_call x1, Pallas kernels, make_filters(): pl.pallas_call(functools.partial(filter_kernel, nd, ns, inner, float(time...  40 us
    dot_general x1, matrix products, local(): jnp.dot(filters.reshape(3 * dipoles, sensors), samples, preferred_element...  6.52 us

profile of v1, /device:TPU:0, one launch (start us, length us, event | category | flops | bytes accessed | tf_op | source)
XLA Modules:
  0.0 92.4 jit_solution(13366745879361053822)
XLA Ops:
  0.0 0.0 copy-start
  0.0 1.1 %select_reduce_fusion = f32[15360]{0:T(1024)S(1)} fusion(f32[3]{0:T(128)} %param.11, s32[15360]{0:T(1024)} %param.10), kind=kLoop, calls=%fused_computation.5 | loop fusion | flops 122880 | bytes 122892 | tf_op jit(solution)/shard_map/reduce_sum | solution.py:33
  1.1 0.8 copy.12
  1.9 0.0 copy-done
  1.9 1.6 %fusion.1.dip = f32[256,3]{1,0:T(8,128)} fusion(f32[3,256]{0,1:T(8,128)S(1)} %copy.12, f32[3,64]{1,0:T(4,128)S(1)} %copy-done, s32[256]{0:T(256)} %param.13), kind=kOutput, calls=%fused_computation.3 | convolution fusion | flops 623360 | bytes 7936 | tf_op jit(solution)/shard_map/dot_general | solution.py:27
  3.5 1.8 %pad_maximum_fusion.node = f32[4,15360]{1,0:T(4,128)} fusion(f32[1,15360]{1,0:T(1,128)S(1)} %bitcast.14, f32[3,15360]{1,0:T(4,128)} %param.9), kind=kLoop, calls=%fused_computation.4 | loop fusion | flops 61440 | bytes 491520 | tf_op jit(solution)/shard_map/concatenate | solution.py:372
  5.3 40.6 %lead_cross.1 = (f32[384,384]{1,0:T(8,128)}, f32[4,3,64,384]{3,2,1,0:T(8,128)}) custom-call(bf16[306,384]{1,0:T(8,128)(2,1)} %rec.3, bf16[306,15360]{1,0:T(8,128)(2,1)} %transfer.1, f32[4,15360]{1,0:T(4,128)} %pad_maximum_fusion.node, f32[256,3]{1,0:T(8,128)} %fusion.1.dip), custom_call_target="tpu_custom_call" | custom-call | tf_op jit(solution)/shard_map/lead_cross/pallas_call | solution.py:183
  45.9 40.0 %filters.1 = (bf16[3,4,64,306]{3,2,1,0:T(8,128)(2,1)}, bf16[306,3072]{1,0:T(8,128)(2,1)}) custom-call(f32[384,384]{1,0:T(8,128)} %get-tuple-element.9.cross, f32[4,3,64,384]{3,2,1,0:T(8,128)} %get-tuple-element.10.lead, bf16[306,384]{1,0:T(8,128)(2,1)} %rec.3), custom_call_target="tpu_custom_call" | custom-call | tf_op jit(solution)/shard_map/filters/pallas_call | solution.py:352
  85.9 6.5 %convolution_convert_fusion = bf16[768,3072]{1,0:T(8,128)(2,1)} fusion(bf16[768,306]{1,0:T(8,128)(2,1)} %bitcast.15, bf16[306,3072]{1,0:T(8,128)(2,1)} %get-tuple-element.12), kind=kOutput, calls=%fused_computation | convolution fusion | flops 1446248448 | bytes 7068672 | tf_op jit(solution)/shard_map/dot_general | solution.py:375
Async XLA Ops:
  0.0 1.9 %copy-start = (f32[3,64]{1,0:T(4,128)S(1)}, f32[3,64]{1,0:T(4,128)}, u32[]{:S(2)}) copy-start(f32[3,64]{1,0:T(4,128)} %param.12) | copy-start | bytes 2308

commit v2 on v1

--- a/solution.py
+++ b/solution.py
@@ -22,15 +22,17 @@
 
 
 def place_dipoles(tile_center, dip_tile, dip_offset):
-    tile_ids = jnp.arange(tile_center.shape[1], dtype=jnp.int32)
-    onehot = (tile_ids[:, None] == dip_tile[None, :]).astype(F32)
-    return jnp.dot(tile_center, onehot, precision=lax.Precision.HIGHEST) + dip_offset
+    tiles, dipoles = tile_center.shape[1], dip_tile.shape[1]
+    onehot = (lax.broadcasted_iota(jnp.int32, (tiles, dipoles), 0) == dip_tile).astype(F32)
+    rows = jnp.dot(tile_center, onehot, precision=lax.Precision.HIGHEST, preferred_element_type=F32) + dip_offset
+    return jnp.concatenate([rows, jnp.zeros((128 - rows.shape[0], dipoles), F32)], axis=0).T
 
 
 def layer_scale(node_layer, layer_cond):
-    levels = jnp.arange(layer_cond.shape[0], dtype=jnp.int32)
-    onehot = (node_layer[None, :] == levels[:, None]).astype(F32)
-    return jnp.sum(layer_cond[:, None] * onehot, axis=0)
+    scale = jnp.zeros(node_layer.shape, F32)
+    for level in range(layer_cond.shape[0]):
+        scale = jnp.where(node_layer == level, layer_cond[level], scale)
+    return scale
 
 
 def remote(held, dst, send_sem, recv_sem, **where):
@@ -40,30 +42,32 @@
     )
 
 
-def potential_rows(node, dip, rows):
+def potential_rows(node, scale, dip, rows):
     dipoles = dip.shape[0]
     parts = [[], [], []]
     for first in range(0, dipoles, rows):
         offsets = [node[c : c + 1, :] - dip[first : first + rows, c : c + 1] for c in range(3)]
         q = offsets[0] * offsets[0] + offsets[1] * offsets[1] + offsets[2] * offsets[2] + SOFTENING
         root = lax.rsqrt(q)
-        weights = (node[3:4, :] * root) * (root * root)
+        weights = (scale * root) * (root * root)
         for c in range(3):
             parts[c].append((offsets[c] * weights).astype(BF16))
     return jnp.concatenate(parts[0] + parts[1] + parts[2], axis=0)
 
 
 def lead_kernel(
-    nd, ns, r, stages,
-    rec, transfer, node, dip, cross_out, lead_out,
-    aug, acc, buf, got_a, part, got_b, fin, res,
-    s_a, r_a, s_b, r_b, s_c, r_c, s_d, r_d,
+    nd, ns, inner, r, stages,
+    rec, transfer, node, layer, cond, centre, tile, offset, cross_out, lead_out, z_out,
+    dip, aug, acc, buf, got_a, part, got_b, fin, res,
+    s_a, r_a, s_b, r_b, s_c, r_c, s_d, r_d, s_z, r_z, own_sem,
 ):
     step = pl.program_id(0)
     me_n, me_s = lax.axis_index("node"), lax.axis_index("src")
     sensors = rec.shape[0]
     dipoles = dip.shape[0]
     mp = aug.shape[0]
+    outer = ns // inner
+    hi, lo = me_s // inner, lax.rem(me_s, inner)
     peer_n = [None] + [lax.rem(me_n + k, nd) for k in range(1, nd)]
     peer_s = [None] + [lax.rem(me_s + k, ns) for k in range(1, ns)]
 
@@ -78,6 +82,12 @@
 
     def copy_d(k):
         return remote(res.at[me_n], res.at[me_n], s_d.at[k - 1], r_d.at[k - 1], node=peer_n[k])
+
+    def copy_z(k):
+        peer = lax.rem(hi + k, outer) * inner + lo
+        return remote(rec, z_out.at[hi], s_z.at[k - 1], r_z.at[k - 1], src=peer)
+
+    keep = pltpu.make_async_copy(rec, z_out.at[hi], own_sem)
 
     @pl.when(step == stages[0])
     def _():
@@ -98,26 +108,24 @@
                 first = (n * ns + s) * r
                 buf[n, s] = cross[first : first + r, :]
         pl.semaphore_wait(barrier, nd - 1 + ns - 1)
-
-    @pl.when(step == stages[1])
-    def _():
         for k in range(1, nd):
             copy_a(k).start()
-
-    @pl.when(step == stages[2])
+        keep.start()
+        for k in range(1, outer, 2):
+            copy_z(k).start()
+        dip[...] = place_dipoles(centre[...], tile[...], offset[...])
+
+    @pl.when(step == stages[1])
     def _():
         total = buf[me_n]
         for k in range(1, nd):
             copy_a(k).wait()
             total = total + got_a[k - 1]
         part[...] = total
-
-    @pl.when(step == stages[3])
-    def _():
         for k in range(1, ns):
             copy_b(k).start()
 
-    @pl.when(step == stages[4])
+    @pl.when(step == stages[2])
     def _():
         total = part[me_s]
         for k in range(1, ns):
@@ -125,13 +133,12 @@
             total = total + got_b[k - 1]
         fin[...] = total
         res[me_n, me_s] = total
-
-    @pl.when(step == stages[5])
-    def _():
         for k in range(1, ns):
             copy_c(k).start()
-
-    @pl.when(step == stages[6])
+        for k in range(2, outer, 2):
+            copy_z(k).start()
+
+    @pl.when(step == stages[3])
     def _():
         for k in range(1, ns):
             copy_c(k).wait()
@@ -141,16 +148,19 @@
     block = transfer.shape[1]
     sub = math.gcd(block, 512)
     dip_now = dip[...]
+    scale = layer_scale(layer[...], cond)
     total = None
     for first in range(0, block, sub):
-        potential = potential_rows(node[:, first : first + sub], dip_now, 32)
+        potential = potential_rows(
+            node[:, first : first + sub], scale[:, first : first + sub], dip_now, 32
+        )
         product = lax.dot_general(
             transfer[:, first : first + sub], potential, NT, preferred_element_type=F32
         )
         total = product if total is None else total + product
     acc[:sensors, :] += total
 
-    @pl.when(step == stages[7])
+    @pl.when(step == stages[4])
     def _():
         flipped = acc[...].T
         own = dipoles // nd
@@ -165,36 +175,46 @@
             for s in range(ns):
                 first = (n * ns + s) * r
                 cross_out[first : first + r, :] = res[n, s]
-
-
-def lead_and_cross(rec, transfer, node, dip):
+        keep.wait()
+        for k in range(1, outer):
+            copy_z(k).wait()
+
+
+def lead_and_cross(inner, rec, transfer, node, layer, cond, centre, tile, offset):
     nd, ns = lax.axis_size("node"), lax.axis_size("src")
     sensors, time = rec.shape
     nodes = transfer.shape[1]
-    dipoles = dip.shape[0]
+    dipoles = tile.shape[1]
+    outer = ns // inner
     mp = round_up(sensors + 1, 128)
     r = -(-(sensors + 1) // (nd * ns))
     block = math.gcd(nodes, 1024)
     steps = nodes // block
     last = steps - 1
-    stages = (0, 1, last * 4 // 14, last * 5 // 14, last * 8 // 14, last * 9 // 14, last * 12 // 14, last)
+    stages = (0, last * 4 // 14, last * 8 // 14, last * 11 // 14, last)
     chunk = (nd, ns, r, mp)
     vmem = pl.BlockSpec(memory_space=pltpu.VMEM)
     return pl.pallas_call(
-        functools.partial(lead_kernel, nd, ns, r, stages),
+        functools.partial(lead_kernel, nd, ns, inner, r, stages),
         grid=(steps,),
         out_shape=(
             jax.ShapeDtypeStruct((mp, mp), F32),
             jax.ShapeDtypeStruct((nd, 3, dipoles // nd, mp), F32),
+            jax.ShapeDtypeStruct((outer, sensors, time), BF16),
         ),
         in_specs=[
             vmem,
             pl.BlockSpec((sensors, block), lambda i: (0, i)),
-            pl.BlockSpec((4, block), lambda i: (0, i)),
+            pl.BlockSpec((3, block), lambda i: (0, i)),
+            pl.BlockSpec((1, block), lambda i: (0, i)),
+            pl.BlockSpec(memory_space=pltpu.SMEM),
+            vmem,
+            vmem,
             vmem,
         ],
-        out_specs=(vmem, vmem),
+        out_specs=(vmem, vmem, pl.BlockSpec(memory_space=pl.ANY)),
         scratch_shapes=[
+            pltpu.VMEM((dipoles, 128), F32),
             pltpu.VMEM((mp, time), BF16),
             pltpu.VMEM((mp, 3 * dipoles), F32),
             pltpu.VMEM(chunk, F32),
@@ -204,10 +224,11 @@
             pltpu.VMEM(chunk[2:], F32),
             pltpu.VMEM(chunk, F32),
         ]
-        + [pltpu.SemaphoreType.DMA((n,)) for n in (nd - 1, nd - 1, ns - 1, ns - 1, ns - 1, ns - 1, nd - 1, nd - 1)],
+        + [pltpu.SemaphoreType.DMA((n,)) for n in (nd - 1, nd - 1, ns - 1, ns - 1, ns - 1, ns - 1, nd - 1, nd - 1, outer - 1, outer - 1)]
+        + [pltpu.SemaphoreType.DMA],
         compiler_params=pltpu.CompilerParams(collective_id=0, has_side_effects=True),
         name="lead_cross",
-    )(rec, transfer, node, dip)
+    )(rec, transfer, node, layer, cond, centre, tile, offset)
 
 
 def dot_full(a, b):
@@ -260,18 +281,16 @@
 
 def filter_kernel(
     nd, ns, inner, count,
-    cross, lead, rec, filt, rec_all,
-    got, s_l, r_l, s_y, r_y, s_z, r_z, s_f, r_f,
+    cross, lead, held, filt, rec_all,
+    got, s_l, r_l, s_y, r_y, s_f, r_f,
 ):
     me_n, me_s = lax.axis_index("node"), lax.axis_index("src")
     outer = ns // inner
-    sensors, time = rec.shape
+    sensors, time = held.shape[1:]
     own = lead.shape[2]
     mp = cross.shape[0]
     hi, lo = me_s // inner, lax.rem(me_s, inner)
     peer_n = [None] + [lax.rem(me_n + k, nd) for k in range(1, nd)]
-    peer_z = [None] + [lax.rem(hi + k, outer) * inner + lo for k in range(1, outer)]
-    from_z = [me_s] + [lax.rem(hi + outer - k, outer) * inner + lo for k in range(1, outer)]
     peer_y = hi * inner + lax.rem(lo + 1, inner)
 
     def columns(s):
@@ -281,11 +300,7 @@
         return remote(lead.at[peer_n[k]], got.at[k - 1], s_l.at[k - 1], r_l.at[k - 1], node=peer_n[k])
 
     def copy_y(k):
-        source = rec if k == 0 else columns(from_z[k])
-        return remote(source, columns(from_z[k]), s_y.at[k], r_y.at[k], src=peer_y)
-
-    def copy_z(k):
-        return remote(rec, columns(me_s), s_z.at[k - 1], r_z.at[k - 1], src=peer_z[k])
+        return remote(held.at[k], columns(k * inner + lo), s_y.at[k], r_y.at[k], src=peer_y)
 
     def copy_f(k):
         return remote(filt.at[:, me_n], filt.at[:, me_n], s_f.at[k - 1], r_f.at[k - 1], node=peer_n[k])
@@ -293,23 +308,19 @@
     barrier = pltpu.get_barrier_semaphore()
     for k in range(1, nd):
         pl.semaphore_signal(barrier, inc=1, device_id={"node": peer_n[k]}, device_id_type=pl.DeviceIdType.MESH)
-    for k in range(1, outer):
-        pl.semaphore_signal(barrier, inc=1, device_id={"src": peer_z[k]}, device_id_type=pl.DeviceIdType.MESH)
     pl.semaphore_signal(barrier, inc=1, device_id={"src": peer_y}, device_id_type=pl.DeviceIdType.MESH)
-    pl.semaphore_wait(barrier, nd - 1 + outer)
+    pl.semaphore_wait(barrier, nd - 1 + 1)
 
     for k in range(1, nd):
         copy_l(k).start()
-    copy_y(0).start()
-    for k in range(1, outer):
-        copy_z(k).start()
-    rec_all[:, pl.ds(pl.multiple_of(me_s * time, time), time)] = rec[...]
-
-    inverse = covariance_inverse(cross[...], sensors, count, 3)
-
-    for k in range(1, outer):
-        copy_z(k).wait()
+    for k in range(outer):
         copy_y(k).start()
+    for k in range(outer):
+        first = pl.multiple_of((k * inner + lo) * time, time)
+        rec_all[:, pl.ds(first, time)] = held[k]
+
+    inverse = covariance_inverse(cross[...], sensors, count, 2)
+
     field = lead[me_n]
     for k in range(1, nd):
         copy_l(k).wait()
@@ -342,11 +353,10 @@
         copy_f(k).wait()
 
 
-def make_filters(cross, lead, rec):
+def make_filters(inner, cross, lead, held):
     nd, ns = lax.axis_size("node"), lax.axis_size("src")
-    sensors, time = rec.shape
+    sensors, time = held.shape[1:]
     own, mp = lead.shape[2:]
-    inner = 2
     outer = ns // inner
     vmem = pl.BlockSpec(memory_space=pltpu.VMEM)
     return pl.pallas_call(
@@ -358,20 +368,20 @@
         in_specs=[vmem] * 3,
         out_specs=(vmem, vmem),
         scratch_shapes=[pltpu.VMEM((nd - 1,) + lead.shape[1:], F32)]
-        + [pltpu.SemaphoreType.DMA((n,)) for n in (nd - 1, nd - 1, outer, outer, outer - 1, outer - 1, nd - 1, nd - 1)],
+        + [pltpu.SemaphoreType.DMA((n,)) for n in (nd - 1, nd - 1, outer, outer, nd - 1, nd - 1)],
         compiler_params=pltpu.CompilerParams(collective_id=1, has_side_effects=True),
         name="filters",
-    )(cross, lead, rec)
+    )(cross, lead, held)
 
 
 def local(transfer, node_pos, node_layer, layer_cond, tile_center, dip_tile, dip_offset, recording):
     sensors = transfer.shape[0]
     dipoles = dip_tile.shape[0]
-    dip_pos = place_dipoles(tile_center, dip_tile, dip_offset)
-    scales = layer_scale(node_layer, layer_cond)
-    node = jnp.concatenate([node_pos, scales[None, :]], axis=0)
-    cross, lead = lead_and_cross(recording, transfer, node, dip_pos.T)
-    filters, samples = make_filters(cross, lead, recording)
+    inner = math.gcd(lax.axis_size("src"), 2)
+    cross, lead, held = lead_and_cross(
+        inner, recording, transfer, node_pos, node_layer[None, :], layer_cond, tile_center, dip_tile[None, :], dip_offset
+    )
+    filters, samples = make_filters(inner, cross, lead, held)
     out = jnp.dot(filters.reshape(3 * dipoles, sensors), samples, preferred_element_type=F32)
     return out.astype(BF16).reshape(3, dipoles, samples.shape[1])
 

time: 92.9 us -> 78.3 us (0.84)
  the two profiles are of different devices: /device:TPU:0 before, /device:TPU:25 now
where the time goes in v2:
time: 78.3 us; the launch traced here: 78.1 us
  Pallas kernels  71.5 us (91%)
  matrix products  6.52 us (8%)
    pallas_call x1, Pallas kernels, lead_and_cross(): pl.pallas_call(functools.partial(lead_kernel, nd, ns, inner, r, stages),...  43.1 us
    pallas_call x1, Pallas kernels, make_filters(): pl.pallas_call(functools.partial(filter_kernel, nd, ns, inner, float(time...  28.4 us
    dot_general x1, matrix products, local(): jnp.dot(filters.reshape(3 * dipoles, sensors), samples, preferred_element...  6.52 us

profile of v2, /device:TPU:25, one launch (start us, length us, event | category | flops | bytes accessed | tf_op | source)
XLA Modules:
  0.0 78.1 jit_solution(15040375118434105754)
XLA Ops:
  0.0 43.1 %lead_cross.1 = (f32[384,384]{1,0:T(8,128)}, f32[4,3,64,384]{3,2,1,0:T(8,128)}, bf16[4,306,384]{2,1,0:T(8,128)(2,1)}) custom-call(bf16[306,384]{1,0:T(8,128)(2,1)} %rec.1, bf16[306,15360]{1,0:T(8,128)(2,1)} %transfer.1, f32[3,15360]{1,0:T(4,128)} %node.1, s32[1,15360]{1,0:T(1,128)} %bitcast.6, f32[3]{0:T(128)} %cond.1, f32[3,64]{1,0:T(4,128)} %centre.1, ...), custom_call_target="tpu_custom_call" | custom-call | tf_op jit(solution)/shard_map/lead_cross/pallas_call | solution.py:197
  43.1 28.4 %filters.1 = (bf16[3,4,64,306]{3,2,1,0:T(8,128)(2,1)}, bf16[306,3072]{1,0:T(8,128)(2,1)}) custom-call(f32[384,384]{1,0:T(8,128)} %get-tuple-element.10.cross, f32[4,3,64,384]{3,2,1,0:T(8,128)} %get-tuple-element.11.lead, bf16[4,306,384]{2,1,0:T(8,128)(2,1)} %get-tuple-element.12.held), custom_call_target="tpu_custom_call" | custom-call | tf_op jit(solution)/shard_map/filters/pallas_call | solution.py:362
  71.5 6.5 %convolution_convert_fusion = bf16[768,3072]{1,0:T(8,128)(2,1)} fusion(bf16[768,306]{1,0:T(8,128)(2,1)} %bitcast.8, bf16[306,3072]{1,0:T(8,128)(2,1)} %get-tuple-element.14), kind=kOutput, calls=%fused_computation | convolution fusion | flops 1446248448 | bytes 7068672 | tf_op jit(solution)/shard_map/dot_general | solution.py:385

commit v3 on v2

--- a/solution.py
+++ b/solution.py
@@ -55,11 +55,38 @@
     return jnp.concatenate(parts[0] + parts[1] + parts[2], axis=0)
 
 
+def pack_halves(aug, half):
+    width = aug.shape[0]
+    second = aug[half : 2 * half]
+    turned = jnp.concatenate([second, aug[:half], aug[2 * half :]], axis=0)
+    top = lax.dot_general(aug[:half], aug, NT, preferred_element_type=F32)
+    low = lax.dot_general(second, turned, NT, preferred_element_type=F32)
+    rows = lax.broadcasted_iota(jnp.int32, (half, width), 0)
+    cols = lax.broadcasted_iota(jnp.int32, (half, width), 1)
+    diagonal = jnp.sum(jnp.where(rows == cols, low, 0.0), axis=1, keepdims=True)
+    packed = jnp.where(cols >= rows, top, low)
+    return jnp.where(cols == 2 * half, diagonal, packed)
+
+
+def unpack_halves(packed):
+    half, width = packed.shape
+    flipped = jnp.concatenate([packed, jnp.zeros((width - half, width), F32)], axis=0).T
+    rows = lax.broadcasted_iota(jnp.int32, (half, width), 0)
+    cols = lax.broadcasted_iota(jnp.int32, (half, width), 1)
+    top = jnp.where(cols >= rows, packed, flipped[:half])
+    top = jnp.where(cols < 2 * half, top, 0.0)
+    corner = jnp.where(rows > cols, packed, flipped[:half])
+    corner = jnp.where(rows == cols, packed[:, 2 * half : 2 * half + 1], corner)
+    corner = jnp.where(cols < half, corner, 0.0)
+    low = jnp.where(cols < half, flipped[half : 2 * half], pltpu.roll(corner, half, 1))
+    return jnp.concatenate([top, low, jnp.zeros((width - 2 * half, width), F32)], axis=0)
+
+
 def lead_kernel(
-    nd, ns, inner, r, stages,
+    nd, ns, inner, half, r, stages,
     rec, transfer, node, layer, cond, centre, tile, offset, cross_out, lead_out, z_out,
     dip, aug, acc, buf, got_a, part, got_b, fin, res,
-    s_a, r_a, s_b, r_b, s_c, r_c, s_d, r_d, s_z, r_z, own_sem,
+    s_a, r_a, s_b, r_b, s_c, r_c, s_d, r_d, s_z, r_z,
 ):
     step = pl.program_id(0)
     me_n, me_s = lax.axis_index("node"), lax.axis_index("src")
@@ -83,11 +110,7 @@
     def copy_d(k):
         return remote(res.at[me_n], res.at[me_n], s_d.at[k - 1], r_d.at[k - 1], node=peer_n[k])
 
-    def copy_z(k):
-        peer = lax.rem(hi + k, outer) * inner + lo
-        return remote(rec, z_out.at[hi], s_z.at[k - 1], r_z.at[k - 1], src=peer)
-
-    keep = pltpu.make_async_copy(rec, z_out.at[hi], own_sem)
+    copy_z = remote(rec, z_out, s_z, r_z, src=lax.rem(hi + 1, outer) * inner + lo)
 
     @pl.when(step == stages[0])
     def _():
@@ -101,18 +124,18 @@
         tail = lax.broadcasted_iota(jnp.int32, (mp - low, aug.shape[1]), 0) + low
         aug[low:, :] = jnp.where(tail == sensors, 1.0, 0.0).astype(BF16)
         aug[:sensors, :] = rec[...]
-        held = aug[...]
-        cross = lax.dot_general(held, held, NT, preferred_element_type=F32)
+        packed = pack_halves(aug[...], half)
+        rows = nd * ns * r
+        if rows > half:
+            packed = jnp.concatenate([packed, jnp.zeros((rows - half, mp), F32)], axis=0)
         for n in range(nd):
             for s in range(ns):
                 first = (n * ns + s) * r
-                buf[n, s] = cross[first : first + r, :]
+                buf[n, s] = packed[first : first + r, :]
         pl.semaphore_wait(barrier, nd - 1 + ns - 1)
         for k in range(1, nd):
             copy_a(k).start()
-        keep.start()
-        for k in range(1, outer, 2):
-            copy_z(k).start()
+        copy_z.start()
         dip[...] = place_dipoles(centre[...], tile[...], offset[...])
 
     @pl.when(step == stages[1])
@@ -135,8 +158,6 @@
         res[me_n, me_s] = total
         for k in range(1, ns):
             copy_c(k).start()
-        for k in range(2, outer, 2):
-            copy_z(k).start()
 
     @pl.when(step == stages[3])
     def _():
@@ -170,14 +191,11 @@
                 lead_out[n, c] = flipped[first : first + own, :]
         for k in range(1, nd):
             copy_d(k).wait()
-        cross_out[...] = jnp.zeros_like(cross_out)
         for n in range(nd):
             for s in range(ns):
                 first = (n * ns + s) * r
                 cross_out[first : first + r, :] = res[n, s]
-        keep.wait()
-        for k in range(1, outer):
-            copy_z(k).wait()
+        copy_z.wait()
 
 
 def lead_and_cross(inner, rec, transfer, node, layer, cond, centre, tile, offset):
@@ -186,8 +204,9 @@
     nodes = transfer.shape[1]
     dipoles = tile.shape[1]
     outer = ns // inner
-    mp = round_up(sensors + 1, 128)
-    r = -(-(sensors + 1) // (nd * ns))
+    half = round_up(-(-(sensors + 1) // 2), 16)
+    mp = round_up(2 * half + 1, 128)
+    r = -(-half // (nd * ns))
     block = math.gcd(nodes, 1024)
     steps = nodes // block
     last = steps - 1
@@ -195,12 +214,12 @@
     chunk = (nd, ns, r, mp)
     vmem = pl.BlockSpec(memory_space=pltpu.VMEM)
     return pl.pallas_call(
-        functools.partial(lead_kernel, nd, ns, inner, r, stages),
+        functools.partial(lead_kernel, nd, ns, inner, half, r, stages),
         grid=(steps,),
         out_shape=(
-            jax.ShapeDtypeStruct((mp, mp), F32),
+            jax.ShapeDtypeStruct((nd * ns * r, mp), F32),
             jax.ShapeDtypeStruct((nd, 3, dipoles // nd, mp), F32),
-            jax.ShapeDtypeStruct((outer, sensors, time), BF16),
+            jax.ShapeDtypeStruct((sensors, time), BF16),
         ),
         in_specs=[
             vmem,
@@ -224,8 +243,8 @@
             pltpu.VMEM(chunk[2:], F32),
             pltpu.VMEM(chunk, F32),
         ]
-        + [pltpu.SemaphoreType.DMA((n,)) for n in (nd - 1, nd - 1, ns - 1, ns - 1, ns - 1, ns - 1, nd - 1, nd - 1, outer - 1, outer - 1)]
-        + [pltpu.SemaphoreType.DMA],
+        + [pltpu.SemaphoreType.DMA((n,)) for n in (nd - 1, nd - 1, ns - 1, ns - 1, ns - 1, ns - 1, nd - 1, nd - 1)]
+        + [pltpu.SemaphoreType.DMA] * 2,
         compiler_params=pltpu.CompilerParams(collective_id=0, has_side_effects=True),
         name="lead_cross",
     )(rec, transfer, node, layer, cond, centre, tile, offset)
@@ -246,7 +265,7 @@
     return dot(ah, bh) + (dot(ah, bl) + dot(al, bh))
 
 
-def covariance_inverse(cross, sensors, count, full_steps):
+def covariance_inverse(cross, sensors, count, full_steps, midway):
     mp = cross.shape[0]
     rows = lax.broadcasted_iota(jnp.int32, (mp, mp), 0)
     cols = lax.broadcasted_iota(jnp.int32, (mp, mp), 1)
@@ -269,6 +288,8 @@
     x = (4.0 * plan[0]) * eye - (2.0 * plan[0]) * scaled
     scaled_halves = halves(scaled)
     for at, gain in enumerate(plan[1:], 1):
+        if at == len(plan) - full_steps:
+            midway()
         if at >= len(plan) - full_steps:
             y = dot_full(scaled, x)
             x = dot_full(x, (4.0 * gain) * eye - (2.0 * gain) * y)
@@ -281,16 +302,18 @@
 
 def filter_kernel(
     nd, ns, inner, count,
-    cross, lead, held, filt, rec_all,
-    got, s_l, r_l, s_y, r_y, s_f, r_f,
+    cross, lead, rec, near, filt, rec_all,
+    got, s_l, r_l, s_y, r_y, s_z, r_z, s_f, r_f,
 ):
     me_n, me_s = lax.axis_index("node"), lax.axis_index("src")
     outer = ns // inner
-    sensors, time = held.shape[1:]
+    sensors, time = rec.shape
     own = lead.shape[2]
-    mp = cross.shape[0]
+    mp = cross.shape[1]
     hi, lo = me_s // inner, lax.rem(me_s, inner)
     peer_n = [None] + [lax.rem(me_n + k, nd) for k in range(1, nd)]
+    peer_z = [None] + [lax.rem(hi + k, outer) * inner + lo for k in range(1, outer)]
+    from_z = [me_s] + [lax.rem(hi + outer - k, outer) * inner + lo for k in range(1, outer)]
     peer_y = hi * inner + lax.rem(lo + 1, inner)
 
     def columns(s):
@@ -300,7 +323,16 @@
         return remote(lead.at[peer_n[k]], got.at[k - 1], s_l.at[k - 1], r_l.at[k - 1], node=peer_n[k])
 
     def copy_y(k):
-        return remote(held.at[k], columns(k * inner + lo), s_y.at[k], r_y.at[k], src=peer_y)
+        source = rec if k == 0 else near if k == 1 else columns(from_z[k])
+        return remote(source, columns(from_z[k]), s_y.at[k], r_y.at[k], src=peer_y)
+
+    def copy_z(k):
+        return remote(rec, columns(me_s), s_z.at[k - 2], r_z.at[k - 2], src=peer_z[k])
+
+    def relay(ks):
+        for k in ks:
+            copy_z(k).wait()
+            copy_y(k).start()
 
     def copy_f(k):
         return remote(filt.at[:, me_n], filt.at[:, me_n], s_f.at[k - 1], r_f.at[k - 1], node=peer_n[k])
@@ -308,18 +340,27 @@
     barrier = pltpu.get_barrier_semaphore()
     for k in range(1, nd):
         pl.semaphore_signal(barrier, inc=1, device_id={"node": peer_n[k]}, device_id_type=pl.DeviceIdType.MESH)
+    for k in range(1, outer):
+        pl.semaphore_signal(barrier, inc=1, device_id={"src": peer_z[k]}, device_id_type=pl.DeviceIdType.MESH)
     pl.semaphore_signal(barrier, inc=1, device_id={"src": peer_y}, device_id_type=pl.DeviceIdType.MESH)
-    pl.semaphore_wait(barrier, nd - 1 + 1)
+    pl.semaphore_wait(barrier, nd - 1 + outer)
 
     for k in range(1, nd):
         copy_l(k).start()
-    for k in range(outer):
+    for k in range(2):
         copy_y(k).start()
-    for k in range(outer):
-        first = pl.multiple_of((k * inner + lo) * time, time)
-        rec_all[:, pl.ds(first, time)] = held[k]
-
-    inverse = covariance_inverse(cross[...], sensors, count, 2)
+    later = list(range(outer - 1, 1, -1))
+    for k in later:
+        copy_z(k).start()
+    for k, block in enumerate((rec, near)):
+        rec_all[:, pl.ds(pl.multiple_of(from_z[k] * time, time), time)] = block[...]
+
+    half = round_up(-(-(sensors + 1) // 2), 16)
+    split = len(later) // 2
+    inverse = covariance_inverse(
+        unpack_halves(cross[:half, :]), sensors, count, 2, functools.partial(relay, later[:split])
+    )
+    relay(later[split:])
 
     field = lead[me_n]
     for k in range(1, nd):
@@ -353,9 +394,9 @@
         copy_f(k).wait()
 
 
-def make_filters(inner, cross, lead, held):
+def make_filters(inner, cross, lead, rec, near):
     nd, ns = lax.axis_size("node"), lax.axis_size("src")
-    sensors, time = held.shape[1:]
+    sensors, time = rec.shape
     own, mp = lead.shape[2:]
     outer = ns // inner
     vmem = pl.BlockSpec(memory_space=pltpu.VMEM)
@@ -365,23 +406,23 @@
             jax.ShapeDtypeStruct((3, nd, own, sensors), BF16),
             jax.ShapeDtypeStruct((sensors, ns * time), BF16),
         ),
-        in_specs=[vmem] * 3,
+        in_specs=[vmem] * 4,
         out_specs=(vmem, vmem),
         scratch_shapes=[pltpu.VMEM((nd - 1,) + lead.shape[1:], F32)]
-        + [pltpu.SemaphoreType.DMA((n,)) for n in (nd - 1, nd - 1, outer, outer, nd - 1, nd - 1)],
+        + [pltpu.SemaphoreType.DMA((n,)) for n in (nd - 1, nd - 1, outer, outer, outer - 2, outer - 2, nd - 1, nd - 1)],
         compiler_params=pltpu.CompilerParams(collective_id=1, has_side_effects=True),
         name="filters",
-    )(cross, lead, held)
+    )(cross, lead, rec, near)
 
 
 def local(transfer, node_pos, node_layer, layer_cond, tile_center, dip_tile, dip_offset, recording):
     sensors = transfer.shape[0]
     dipoles = dip_tile.shape[0]
     inner = math.gcd(lax.axis_size("src"), 2)
-    cross, lead, held = lead_and_cross(
+    cross, lead, near = lead_and_cross(
         inner, recording, transfer, node_pos, node_layer[None, :], layer_cond, tile_center, dip_tile[None, :], dip_offset
     )
-    filters, samples = make_filters(inner, cross, lead, held)
+    filters, samples = make_filters(inner, cross, lead, recording, near)
     out = jnp.dot(filters.reshape(3 * dipoles, sensors), samples, preferred_element_type=F32)
     return out.astype(BF16).reshape(3, dipoles, samples.shape[1])
 

time: 78.3 us -> 68.6 us (0.88)
  the two profiles are of different devices: /device:TPU:25 before, /device:TPU:0 now
where the time goes in v3:
time: 68.6 us; the launch traced here: 68.4 us
  Pallas kernels  61.9 us (90%)
  matrix products  6.52 us (10%)
    pallas_call x1, Pallas kernels, make_filters(): pl.pallas_call(functools.partial(filter_kernel, nd, ns, inner, float(time...  33.1 us
    pallas_call x1, Pallas kernels, lead_and_cross(): pl.pallas_call(functools.partial(lead_kernel, nd, ns, inner, half, r, sta...  28.8 us
    dot_general x1, matrix products, local(): jnp.dot(filters.reshape(3 * dipoles, sensors), samples, preferred_element...  6.52 us

profile of v3, /device:TPU:0, one launch (start us, length us, event | category | flops | bytes accessed | tf_op | source)
XLA Modules:
  0.0 68.4 jit_solution(8105505973823317344)
XLA Ops:
  0.0 28.8 %lead_cross.1 = (f32[160,384]{1,0:T(8,128)}, f32[4,3,64,384]{3,2,1,0:T(8,128)}, bf16[306,384]{1,0:T(8,128)(2,1)}) custom-call(bf16[306,384]{1,0:T(8,128)(2,1)} %rec.3, bf16[306,15360]{1,0:T(8,128)(2,1)} %transfer.1, f32[3,15360]{1,0:T(4,128)} %node.1, s32[1,15360]{1,0:T(1,128)} %bitcast.6, f32[3]{0:T(128)} %cond.1, f32[3,64]{1,0:T(4,128)} %centre.1, ...), custom_call_target="tpu_custom_call" | custom-call | tf_op jit(solution)/shard_map/lead_cross/pallas_call | solution.py:216
  28.8 33.1 %filters.1 = (bf16[3,4,64,306]{3,2,1,0:T(8,128)(2,1)}, bf16[306,3072]{1,0:T(8,128)(2,1)}) custom-call(f32[160,384]{1,0:T(8,128)} %get-tuple-element.10.cross, f32[4,3,64,384]{3,2,1,0:T(8,128)} %get-tuple-element.11.lead, bf16[306,384]{1,0:T(8,128)(2,1)} %rec.3, bf16[306,384]{1,0:T(8,128)(2,1)} %get-tuple-element.12.near), custom_call_target="tpu_custom_call" | custom-call | tf_op jit(solution)/shard_map/filters/pallas_call | solution.py:403
  61.9 6.5 %convolution_convert_fusion = bf16[768,3072]{1,0:T(8,128)(2,1)} fusion(bf16[768,306]{1,0:T(8,128)(2,1)} %bitcast.8, bf16[306,3072]{1,0:T(8,128)(2,1)} %get-tuple-element.14), kind=kOutput, calls=%fused_computation | convolution fusion | flops 1446248448 | bytes 7068672 | tf_op jit(solution)/shard_map/dot_general | solution.py:426

commit v4 on v3

--- a/solution.py
+++ b/solution.py
@@ -82,11 +82,15 @@
     return jnp.concatenate([top, low, jnp.zeros((width - 2 * half, width), F32)], axis=0)
 
 
+def near_hops(outer):
+    return sorted({1, outer - 1})
+
+
 def lead_kernel(
     nd, ns, inner, half, r, stages,
     rec, transfer, node, layer, cond, centre, tile, offset, cross_out, lead_out, z_out,
-    dip, aug, acc, buf, got_a, part, got_b, fin, res,
-    s_a, r_a, s_b, r_b, s_c, r_c, s_d, r_d, s_z, r_z,
+    dip, aug, acc, pair, got_p, buf, got_a, part, got_b, fin, res,
+    s_a, r_a, s_b, r_b, s_c, r_c, s_d, r_d, s_z, r_z, s_p, r_p,
 ):
     step = pl.program_id(0)
     me_n, me_s = lax.axis_index("node"), lax.axis_index("src")
@@ -110,7 +114,14 @@
     def copy_d(k):
         return remote(res.at[me_n], res.at[me_n], s_d.at[k - 1], r_d.at[k - 1], node=peer_n[k])
 
-    copy_z = remote(rec, z_out, s_z, r_z, src=lax.rem(hi + 1, outer) * inner + lo)
+    near = near_hops(outer)
+
+    def copy_z(at):
+        peer = lax.rem(hi + near[at], outer) * inner + lo
+        return remote(rec, z_out.at[at], s_z.at[at], r_z.at[at], src=peer)
+
+    core = lax.rem(me_n, 2)
+    copy_p = remote(pair.at[1 - core], got_p, s_p, r_p, node=me_n + 1 - 2 * core)
 
     @pl.when(step == stages[0])
     def _():
@@ -135,7 +146,7 @@
         pl.semaphore_wait(barrier, nd - 1 + ns - 1)
         for k in range(1, nd):
             copy_a(k).start()
-        copy_z.start()
+        copy_z(0).start()
         dip[...] = place_dipoles(centre[...], tile[...], offset[...])
 
     @pl.when(step == stages[1])
@@ -165,6 +176,8 @@
             copy_c(k).wait()
         for k in range(1, nd):
             copy_d(k).start()
+        for at in range(1, len(near)):
+            copy_z(at).start()
 
     block = transfer.shape[1]
     sub = math.gcd(block, 512)
@@ -184,18 +197,22 @@
     @pl.when(step == stages[4])
     def _():
         flipped = acc[...].T
-        own = dipoles // nd
-        for n in range(nd):
+        own = dipoles // 2
+        for n in range(2):
             for c in range(3):
                 first = c * dipoles + n * own
-                lead_out[n, c] = flipped[first : first + own, :]
+                pair[n, c] = flipped[first : first + own, :]
+        copy_p.start()
         for k in range(1, nd):
             copy_d(k).wait()
         for n in range(nd):
             for s in range(ns):
                 first = (n * ns + s) * r
                 cross_out[first : first + r, :] = res[n, s]
-        copy_z.wait()
+        copy_p.wait()
+        lead_out[...] = pair[core] + got_p[...]
+        for at in range(len(near)):
+            copy_z(at).wait()
 
 
 def lead_and_cross(inner, rec, transfer, node, layer, cond, centre, tile, offset):
@@ -218,8 +235,8 @@
         grid=(steps,),
         out_shape=(
             jax.ShapeDtypeStruct((nd * ns * r, mp), F32),
-            jax.ShapeDtypeStruct((nd, 3, dipoles // nd, mp), F32),
-            jax.ShapeDtypeStruct((sensors, time), BF16),
+            jax.ShapeDtypeStruct((3, dipoles // 2, mp), F32),
+            jax.ShapeDtypeStruct((len(near_hops(outer)), sensors, time), BF16),
         ),
         in_specs=[
             vmem,
@@ -236,6 +253,8 @@
             pltpu.VMEM((dipoles, 128), F32),
             pltpu.VMEM((mp, time), BF16),
             pltpu.VMEM((mp, 3 * dipoles), F32),
+            pltpu.VMEM((2, 3, dipoles // 2, mp), F32),
+            pltpu.VMEM((3, dipoles // 2, mp), F32),
             pltpu.VMEM(chunk, F32),
             pltpu.VMEM((nd - 1,) + chunk[1:], F32),
             pltpu.VMEM(chunk[1:], F32),
@@ -244,6 +263,7 @@
             pltpu.VMEM(chunk, F32),
         ]
         + [pltpu.SemaphoreType.DMA((n,)) for n in (nd - 1, nd - 1, ns - 1, ns - 1, ns - 1, ns - 1, nd - 1, nd - 1)]
+        + [pltpu.SemaphoreType.DMA((len(near_hops(outer)),))] * 2
         + [pltpu.SemaphoreType.DMA] * 2,
         compiler_params=pltpu.CompilerParams(collective_id=0, has_side_effects=True),
         name="lead_cross",
@@ -308,10 +328,13 @@
     me_n, me_s = lax.axis_index("node"), lax.axis_index("src")
     outer = ns // inner
     sensors, time = rec.shape
-    own = lead.shape[2]
+    own = lead.shape[1]
     mp = cross.shape[1]
     hi, lo = me_s // inner, lax.rem(me_s, inner)
-    peer_n = [None] + [lax.rem(me_n + k, nd) for k in range(1, nd)]
+    core, chips = lax.rem(me_n, 2), nd // 2
+    peer_x = [None] + [lax.rem(me_n // 2 + k, chips) * 2 + core for k in range(1, chips)]
+    partner = me_n + 1 - 2 * core
+    hops = near_hops(outer)
     peer_z = [None] + [lax.rem(hi + k, outer) * inner + lo for k in range(1, outer)]
     from_z = [me_s] + [lax.rem(hi + outer - k, outer) * inner + lo for k in range(1, outer)]
     peer_y = hi * inner + lax.rem(lo + 1, inner)
@@ -320,50 +343,47 @@
         return rec_all.at[:, pl.ds(pl.multiple_of(s * time, time), time)]
 
     def copy_l(k):
-        return remote(lead.at[peer_n[k]], got.at[k - 1], s_l.at[k - 1], r_l.at[k - 1], node=peer_n[k])
+        return remote(lead, got.at[k - 1], s_l.at[k - 1], r_l.at[k - 1], node=peer_x[k])
 
     def copy_y(k):
-        source = rec if k == 0 else near if k == 1 else columns(from_z[k])
+        source = rec if k == 0 else near.at[hops.index(k)] if k in hops else columns(from_z[k])
         return remote(source, columns(from_z[k]), s_y.at[k], r_y.at[k], src=peer_y)
 
     def copy_z(k):
-        return remote(rec, columns(me_s), s_z.at[k - 2], r_z.at[k - 2], src=peer_z[k])
+        return remote(rec, columns(me_s), s_z.at[k - 1], r_z.at[k - 1], src=peer_z[k])
 
     def relay(ks):
         for k in ks:
             copy_z(k).wait()
             copy_y(k).start()
 
-    def copy_f(k):
-        return remote(filt.at[:, me_n], filt.at[:, me_n], s_f.at[k - 1], r_f.at[k - 1], node=peer_n[k])
+    copy_f = remote(filt.at[:, core], filt.at[:, core], s_f, r_f, node=partner)
 
     barrier = pltpu.get_barrier_semaphore()
-    for k in range(1, nd):
-        pl.semaphore_signal(barrier, inc=1, device_id={"node": peer_n[k]}, device_id_type=pl.DeviceIdType.MESH)
+    for peer in peer_x[1:] + [partner]:
+        pl.semaphore_signal(barrier, inc=1, device_id={"node": peer}, device_id_type=pl.DeviceIdType.MESH)
     for k in range(1, outer):
         pl.semaphore_signal(barrier, inc=1, device_id={"src": peer_z[k]}, device_id_type=pl.DeviceIdType.MESH)
     pl.semaphore_signal(barrier, inc=1, device_id={"src": peer_y}, device_id_type=pl.DeviceIdType.MESH)
-    pl.semaphore_wait(barrier, nd - 1 + outer)
-
-    for k in range(1, nd):
+    pl.semaphore_wait(barrier, chips + outer)
+
+    for k in range(1, chips):
         copy_l(k).start()
-    for k in range(2):
+    for k in [0] + hops:
         copy_y(k).start()
-    later = list(range(outer - 1, 1, -1))
+    later = [k for k in range(1, outer) if k not in hops]
     for k in later:
         copy_z(k).start()
-    for k, block in enumerate((rec, near)):
-        rec_all[:, pl.ds(pl.multiple_of(from_z[k] * time, time), time)] = block[...]
+    for k in [0] + hops:
+        first = pl.multiple_of(from_z[k] * time, time)
+        rec_all[:, pl.ds(first, time)] = rec[...] if k == 0 else near[hops.index(k)]
 
     half = round_up(-(-(sensors + 1) // 2), 16)
-    split = len(later) // 2
     inverse = covariance_inverse(
-        unpack_halves(cross[:half, :]), sensors, count, 2, functools.partial(relay, later[:split])
+        unpack_halves(cross[:half, :]), sensors, count, 2, functools.partial(relay, later)
     )
-    relay(later[split:])
-
-    field = lead[me_n]
-    for k in range(1, nd):
+    field = lead[...]
+    for k in range(1, chips):
         copy_l(k).wait()
         field = field + got[k - 1]
     square = jnp.sum(jnp.sum(field * field, axis=0), axis=1, keepdims=True) / (3.0 * sensors)
@@ -385,31 +405,30 @@
     determinant = gram[0, 0] * cofactor(0, 0) + gram[0, 1] * cofactor(0, 1) + gram[0, 2] * cofactor(0, 2)
     for c in range(3):
         mixed = sum((cofactor(d, c) / determinant) * solved[d] for d in range(3))
-        filt[c, me_n] = mixed[:, :sensors].astype(BF16)
-    for k in range(1, nd):
-        copy_f(k).start()
+        filt[c, core] = mixed[:, :sensors].astype(BF16)
+    copy_f.start()
     for k in range(outer):
         copy_y(k).wait()
-    for k in range(1, nd):
-        copy_f(k).wait()
+    copy_f.wait()
 
 
 def make_filters(inner, cross, lead, rec, near):
     nd, ns = lax.axis_size("node"), lax.axis_size("src")
     sensors, time = rec.shape
-    own, mp = lead.shape[2:]
+    own, mp = lead.shape[1:]
     outer = ns // inner
     vmem = pl.BlockSpec(memory_space=pltpu.VMEM)
     return pl.pallas_call(
         functools.partial(filter_kernel, nd, ns, inner, float(time * nd * ns)),
         out_shape=(
-            jax.ShapeDtypeStruct((3, nd, own, sensors), BF16),
+            jax.ShapeDtypeStruct((3, 2, own, sensors), BF16),
             jax.ShapeDtypeStruct((sensors, ns * time), BF16),
         ),
         in_specs=[vmem] * 4,
         out_specs=(vmem, vmem),
-        scratch_shapes=[pltpu.VMEM((nd - 1,) + lead.shape[1:], F32)]
-        + [pltpu.SemaphoreType.DMA((n,)) for n in (nd - 1, nd - 1, outer, outer, outer - 2, outer - 2, nd - 1, nd - 1)],
+        scratch_shapes=[pltpu.VMEM((max(nd // 2 - 1, 1),) + lead.shape, F32)]
+        + [pltpu.SemaphoreType.DMA((n,)) for n in (max(nd // 2 - 1, 1),) * 2 + (outer,) * 4]
+        + [pltpu.SemaphoreType.DMA] * 2,
         compiler_params=pltpu.CompilerParams(collective_id=1, has_side_effects=True),
         name="filters",
     )(cross, lead, rec, near)

time: 68.6 us -> 66.8 us (0.974)
  Pallas kernels: 61.9 us -> 60 us
    pallas_call x1, Pallas kernels: 33.1 us -> 29.2 us  [make_filters(): pl.pallas_call(functools.partial(filter_kernel, nd, ns, inner, float(time...]
    pallas_call x1, Pallas kernels: 28.8 us -> 30.9 us  [lead_and_cross(): pl.pallas_call(functools.partial(lead_kernel, nd, ns, inner, half, r, sta...]
where the time goes in v4:
time: 66.8 us; the launch traced here: 66.6 us
  Pallas kernels  60 us (90%)
  matrix products  6.52 us (10%)
    pallas_call x1, Pallas kernels, lead_and_cross(): pl.pallas_call(functools.partial(lead_kernel, nd, ns, inner, half, r, sta...  30.9 us
    pallas_call x1, Pallas kernels, make_filters(): pl.pallas_call(functools.partial(filter_kernel, nd, ns, inner, float(time...  29.2 us
    dot_general x1, matrix products, local(): jnp.dot(filters.reshape(3 * dipoles, sensors), samples, preferred_element...  6.52 us

profile of v4, /device:TPU:0, one launch (start us, length us, event | category | flops | bytes accessed | tf_op | source)
XLA Modules:
  0.0 66.6 jit_solution(9695744081491386096)
XLA Ops:
  0.0 30.9 %lead_cross.1 = (f32[160,384]{1,0:T(8,128)}, f32[3,128,384]{2,1,0:T(8,128)}, bf16[2,306,384]{2,1,0:T(8,128)(2,1)}) custom-call(bf16[306,384]{1,0:T(8,128)(2,1)} %rec.3, bf16[306,15360]{1,0:T(8,128)(2,1)} %transfer.1, f32[3,15360]{1,0:T(4,128)} %node.1, s32[1,15360]{1,0:T(1,128)} %bitcast.6, f32[3]{0:T(128)} %cond.1, f32[3,64]{1,0:T(4,128)} %centre.1, ...), custom_call_target="tpu_custom_call" | custom-call | tf_op jit(solution)/shard_map/lead_cross/pallas_call | solution.py:233
  30.9 29.2 %filters.1 = (bf16[3,2,128,306]{3,2,1,0:T(8,128)(2,1)}, bf16[306,3072]{1,0:T(8,128)(2,1)}) custom-call(f32[160,384]{1,0:T(8,128)} %get-tuple-element.10.cross, f32[3,128,384]{2,1,0:T(8,128)} %get-tuple-element.11.lead, bf16[306,384]{1,0:T(8,128)(2,1)} %rec.3, bf16[2,306,384]{2,1,0:T(8,128)(2,1)} %get-tuple-element.12.near), custom_call_target="tpu_custom_call" | custom-call | tf_op jit(solution)/shard_map/filters/pallas_call | solution.py:421
  60.1 6.5 %convolution_convert_fusion = bf16[768,3072]{1,0:T(8,128)(2,1)} fusion(bf16[768,306]{1,0:T(8,128)(2,1)} %bitcast.8, bf16[306,3072]{1,0:T(8,128)(2,1)} %get-tuple-element.14), kind=kOutput, calls=%fused_computation | convolution fusion | flops 1446248448 | bytes 7068672 | tf_op jit(solution)/shard_map/dot_general | solution.py:445

commit v5 on v4

--- a/solution.py
+++ b/solution.py
@@ -169,6 +169,8 @@
         res[me_n, me_s] = total
         for k in range(1, ns):
             copy_c(k).start()
+        for at in range(1, len(near)):
+            copy_z(at).start()
 
     @pl.when(step == stages[3])
     def _():
@@ -176,8 +178,6 @@
             copy_c(k).wait()
         for k in range(1, nd):
             copy_d(k).start()
-        for at in range(1, len(near)):
-            copy_z(at).start()
 
     block = transfer.shape[1]
     sub = math.gcd(block, 512)

time: 66.8 us -> 66.6 us (level)
  no operation moved by 1% of the time
where the time goes in v5:
time: 66.6 us; the launch traced here: 66.4 us
  Pallas kernels  59.8 us (90%)
  matrix products  6.52 us (10%)
    pallas_call x1, Pallas kernels, lead_and_cross(): pl.pallas_call(functools.partial(lead_kernel, nd, ns, inner, half, r, sta...  30.7 us
    pallas_call x1, Pallas kernels, make_filters(): pl.pallas_call(functools.partial(filter_kernel, nd, ns, inner, float(time...  29.1 us
    dot_general x1, matrix products, local(): jnp.dot(filters.reshape(3 * dipoles, sensors), samples, preferred_element...  6.52 us

profile of v5, /device:TPU:0, one launch (start us, length us, event | category | flops | bytes accessed | tf_op | source)
XLA Modules:
  0.0 66.4 jit_solution(11137691175062185847)
XLA Ops:
  0.0 30.7 %lead_cross.1 = (f32[160,384]{1,0:T(8,128)}, f32[3,128,384]{2,1,0:T(8,128)}, bf16[2,306,384]{2,1,0:T(8,128)(2,1)}) custom-call(bf16[306,384]{1,0:T(8,128)(2,1)} %rec.3, bf16[306,15360]{1,0:T(8,128)(2,1)} %transfer.1, f32[3,15360]{1,0:T(4,128)} %node.1, s32[1,15360]{1,0:T(1,128)} %bitcast.6, f32[3]{0:T(128)} %cond.1, f32[3,64]{1,0:T(4,128)} %centre.1, ...), custom_call_target="tpu_custom_call" | custom-call | tf_op jit(solution)/shard_map/lead_cross/pallas_call | solution.py:233
  30.7 29.1 %filters.1 = (bf16[3,2,128,306]{3,2,1,0:T(8,128)(2,1)}, bf16[306,3072]{1,0:T(8,128)(2,1)}) custom-call(f32[160,384]{1,0:T(8,128)} %get-tuple-element.10.cross, f32[3,128,384]{2,1,0:T(8,128)} %get-tuple-element.11.lead, bf16[306,384]{1,0:T(8,128)(2,1)} %rec.3, bf16[2,306,384]{2,1,0:T(8,128)(2,1)} %get-tuple-element.12.near), custom_call_target="tpu_custom_call" | custom-call | tf_op jit(solution)/shard_map/filters/pallas_call | solution.py:421
  59.9 6.5 %convolution_convert_fusion = bf16[768,3072]{1,0:T(8,128)(2,1)} fusion(bf16[768,306]{1,0:T(8,128)(2,1)} %bitcast.8, bf16[306,3072]{1,0:T(8,128)(2,1)} %get-tuple-element.14), kind=kOutput, calls=%fused_computation | convolution fusion | flops 1446248448 | bytes 7068672 | tf_op jit(solution)/shard_map/dot_general | solution.py:445
